TPU v7x, 32 devices: a whole 2x2x4 slice. The times are simulated.
32 devices in a mesh: groups: 2 (over y), seq: 4 (over z), rows: 2 (over x), cfg: 2 (over core).
Axes of the slice: x: 2, y: 2, z: 4, core: 2. Of those that a mesh axis runs over, the one named last changes fastest.
Arguments:
- hidden: bfloat16 [2, 4096, 5120], P('cfg', ('groups', 'seq', 'rows')), parts along dimension 1, may hold values from -500 to 500
- token_order: int32 [4096], P(('groups', 'seq', 'rows')), parts along dimension 0, may hold values from 0 to 2047, as said below
- noisy_latent: float32 [16, 8, 2048], P(('groups', 'seq'), ('rows', 'cfg')), parts along dimension 0, may hold values from -6 to 6
- head_weight: bfloat16 [5120, 64], replicated, may hold values from -0.078125 to 0.078125
- head_mod: float32 [2, 5120], replicated, may hold values from -2.5 to 2.5
- guidance: float32 [1], replicated, may hold values from 3 to 7
- timestep_index: int32 [1], replicated, may hold values from 0 to 7
- step_table: int32 [9], replicated, may hold values from 0 to 1000, as said below
- vae_mean: float32 [16], replicated, may hold values from -2.5 to 2.5
- vae_std: float32 [16], replicated, may hold values from 1.1 to 3.3
- conv2_weight: float32 [16, 16], replicated, may hold values from -1.5 to 1.5
- conv2_bias: float32 [16], replicated, may hold values from -2.5 to 2.5
- conv1_weight: bfloat16 [27, 16, 384], replicated, may hold values from -0.3125 to 0.3125
- conv1_bias: float32 [384], replicated, may hold values from -2.5 to 2.5
Outputs:
- decoded: bfloat16 [16, 8, 128, 384], P(('groups', 'seq'), ('rows', 'cfg')), parts along dimension 0
There are 2 independent parts, one for each index of `groups`. A program takes and returns all parts, laid end to end along the dimension named above; an argument that names none is the same for every part. Nothing has to cross between parts.
Inputs may be any that keep to these rules, and one draw needn't show every extreme that they name: `token_order`: a permutation of the 2048 cells, cell f * 4 * 64 + i * 64 + j being token column j of token row i of frame f; positions k * 256 to (k + 1) * 256 - 1 with k = s * 2 + r hold exactly the cells of frames s * 2 to (s + 1) * 2 - 1 and token rows r * 2 to (r + 1) * 2 - 1. `step_table`: strictly decreasing from 1000 to 0; consecutive entries differ by 90 or more.
All inputs are finite; a program needn't handle non-finite values.
Results may differ from a plain program's by a relative error of at most 0.0053.
Values may be sent and summed in bfloat16 or wider, within the bound.
No kernel may reach another device: no remote copies, remote signals or barrier semaphores. Data moves between devices by JAX's collectives and lax.ppermute only.
A program may use at most 64 MiB of HBM per device.

v0:
```python
import jax
import jax.numpy as jnp
from jax import lax
from jax.sharding import PartitionSpec as P

FR_DEV = 2
TR_DEV = 2
WT = 64


def padded_2(block, sides, width):
    for axis, dim in sides:
        count = lax.axis_size(axis)
        forward = [(i, i + 1) for i in range(count - 1)]
        backward = [(target, source) for source, target in forward]
        low = lax.ppermute(
            lax.slice_in_dim(block, block.shape[dim] - width, None, axis=dim), axis, forward
        )
        high = lax.ppermute(lax.slice_in_dim(block, 0, width, axis=dim), axis, backward)
        block = jnp.concatenate([low, block, high], axis=dim)
    return block


def shifted(block, axis, distance):
    devices = range(lax.axis_size(axis))
    route = [(i - distance, i) for i in devices if i - distance in devices]
    return lax.ppermute(block, axis, route)


def head_rows(row_block, head_weight, head_mod):
    values = row_block.astype(jnp.float32)
    center = jnp.mean(values, axis=-1, keepdims=True)
    spread = jnp.mean(jnp.square(values - center), axis=-1, keepdims=True)
    normed = (values - center) * lax.rsqrt(spread + 1e-06)
    head_in = (normed * (1.0 + head_mod[1]) + head_mod[0]).astype(jnp.bfloat16)
    return jnp.dot(head_in, head_weight, preferred_element_type=jnp.float32)


def conv_taps(padded, frames, row_count, col_count):
    pieces = []
    for step_time in range(3):
        for step_row in range(3):
            for step_col in range(3):
                pieces.append(
                    padded[
                        step_time : step_time + frames,
                        step_row : step_row + row_count,
                        step_col : step_col + col_count,
                        :,
                    ]
                )
    return jnp.concatenate(pieces, axis=-1)


def per_device(
    hidden,
    token_order,
    noisy_latent,
    head_weight,
    head_mod,
    guidance,
    timestep_index,
    step_table,
    vae_mean,
    vae_std,
    conv2_weight,
    conv2_bias,
    conv1_weight,
    conv1_bias,
):
    token_count = hidden.shape[1]
    patch_width = head_weight.shape[1]
    lat_channels = vae_mean.shape[0]
    out_channels = conv1_weight.shape[2]
    token_rows = TR_DEV * lax.axis_size("rows")
    own_head = head_rows(hidden[0], head_weight, head_mod)
    frame_pos = token_order // (token_rows * WT) % FR_DEV
    row_pos = token_order // WT % TR_DEV
    col_pos = token_order % WT
    local_cell = (frame_pos * TR_DEV + row_pos) * WT + col_pos
    placed = jnp.zeros((token_count, patch_width), jnp.float32).at[local_cell].set(own_head)
    local_block = placed.reshape(FR_DEV, TR_DEV, WT, 2, 2, lat_channels).transpose(0, 1, 3, 2, 4, 5)
    local_block = local_block.reshape(FR_DEV, 2, TR_DEV, 2 * WT * lat_channels)
    gathered = lax.all_gather(local_block[None], "cfg", axis=0, tiled=True)
    half_index = lax.axis_index("cfg")
    conditional = lax.dynamic_index_in_dim(gathered[0], half_index, 1, keepdims=False)
    unconditional = lax.dynamic_index_in_dim(gathered[1], half_index, 1, keepdims=False)
    velocity = unconditional + guidance[0] * (conditional - unconditional)
    step_index = timestep_index[0]
    sigma_now = step_table[step_index].astype(jnp.float32) / 1000.0
    sigma_next = step_table[step_index + 1].astype(jnp.float32) / 1000.0
    stepped = noisy_latent + (sigma_next - sigma_now) * velocity
    channels = stepped.reshape(FR_DEV, TR_DEV, 2 * WT, lat_channels) * vae_std + vae_mean
    mixed_lat = (
        jnp.einsum("fyxc,cd->fyxd", channels, conv2_weight, precision=lax.Precision.HIGHEST)
        + conv2_bias
    )
    latent_in = mixed_lat.astype(jnp.bfloat16).reshape(FR_DEV, TR_DEV, 2 * WT * lat_channels)
    framed = padded_2(latent_in, ((("rows", "cfg"), 1),), 1)
    earlier = shifted(framed, "seq", 1)
    padded = jnp.concatenate([earlier, framed], axis=0).reshape(
        FR_DEV + 2, TR_DEV + 2, 2 * WT, lat_channels
    )
    padded = jnp.pad(padded, ((0, 0), (0, 0), (1, 1), (0, 0)))
    tap_columns = conv_taps(padded, FR_DEV, TR_DEV, 2 * WT).reshape(
        FR_DEV * TR_DEV * 2 * WT, 27 * lat_channels
    )
    kernel = conv1_weight.reshape(27 * lat_channels, out_channels)
    result = jnp.dot(tap_columns, kernel, preferred_element_type=jnp.float32) + conv1_bias
    return result.astype(jnp.bfloat16).reshape(FR_DEV, TR_DEV, 2 * WT, out_channels)


def solution(mesh):
    return jax.shard_map(
        per_device,
        mesh=mesh,
        in_specs=(
            P("cfg", ("groups", "seq", "rows"), None),
            P(("groups", "seq", "rows")),
            P(("groups", "seq"), ("rows", "cfg"), None),
            P(),
            P(),
            P(),
            P(),
            P(),
            P(),
            P(),
            P(),
            P(),
            P(),
            P(),
        ),
        out_specs=P(("groups", "seq"), ("rows", "cfg"), None, None),
        check_vma=False,
    )
```

profile of v0, /device:TPU:1, one launch (start us, length us, event | category | flops | bytes accessed | tf_op | source)
XLA Modules:
  0.0 36.1 jit_solution(17837188760740041675)
XLA Ops:
  0.8 1.4 %fusion.30 = (s32[1]{0:T(128)}, s32[1]{0:T(128)}) fusion(s32[9]{0:T(128)} %param.21, s32[]{:T(128)S(6)} %select_n.38, s32[]{:T(128)S(6)} %select_n.37), kind=kLoop, calls=%fused_computation.73 | loop fusion | bytes 24 | tf_op jit(solution)/shard_map/dynamic_slice | solution.py:90
  3.5 0.9 %slice_add_fusion = (f32[1,5120]{1,0:T(1,128)S(1)}, f32[1,5120]{1,0:T(1,128)S(1)}) fusion(f32[2,5120]{1,0:T(2,128)} %param.18), kind=kLoop, calls=%fused_computation.26 | loop fusion | flops 5120 | bytes 81920 | tf_op jit(solution)/shard_map/add | solution.py:35
  4.4 2.2 %convert_reduce_fusion = f32[256]{0:T(256)S(1)} fusion(bf16[1,256,5120]{2,1,0:T(8,128)(2,1)} %param.14), kind=kLoop, calls=%fused_computation.1 | loop fusion | flops 2621184 | bytes 2622464 | tf_op jit(solution)/shard_map/reduce_sum | solution.py:32
  6.6 0.8 %fusion.3 = f32[256]{0:T(256)S(1)} fusion(bf16[1,256,5120]{2,1,0:T(8,128)(2,1)S(1)} %copy-done.1, f32[256]{0:T(256)S(1)} %broadcast_multiply_fusion), kind=kLoop, calls=%fused_computation.6 | loop fusion | flops 5242624 | bytes 2623488 | tf_op jit(solution)/shard_map/reduce_sum | solution.py:33
  7.5 1.1 %fusion.7 = f32[256,64]{1,0:T(8,128)S(1)} fusion(bf16[5120,64]{0,1:T(8,128)(2,1)S(1)} %copy-done, bf16[1,256,5120]{2,1,0:T(8,128)(2,1)S(1)} %copy-done.1, f32[5120]{0:T(1024)S(1)} %bitcast.57, f32[5120]{0:T(1024)S(1)} %bitcast.56, f32[256]{0:T(256)S(1)} %add_rsqrt_fusion, f32[256]{0:T(256)S(1)} %broadcast_multiply_fusion), kind=kOutput, calls=%fused_computation.10 | convolution fusion | flops 175636480 | bytes 3385344 | tf_op jit(solution)/shard_map/dot_general | solution.py:36
  8.7 0.0 copy-start.6
  8.7 0.0 copy-start.7
  8.7 1.2 %scatter_custom_fusion = f32[256,64]{1,0:T(8,128)S(1)} fusion(s32[256]{0:T(256)S(1)} %compare_select_fusion, f32[256,64]{1,0:T(8,128)S(1)} %fusion.7, f32[]{:T(128)} %constant.82.clone.1), kind=kCustom, calls=%fused_computation.16 | custom fusion | bytes 65540 | tf_op jit(solution)/shard_map/scatter | solution.py:81
  9.9 0.1 copy.30
  10.0 0.1 reshape.49
  10.1 0.3 copy.31
  10.4 0.7 %broadcast_in_dim_reshape.3 = f32[1,2,2,2,2048]{4,3,2,1,0:T(2,128)S(1)} reshape(f32[2,2,2,64,2,16]{5,4,3,2,1,0:T(2,128)S(1)} %copy.31) | data formatting | bytes 131072 | tf_op jit(solution)/shard_map/broadcast_in_dim;reshape | solution.py:84
  11.1 1.9 %all_gather.3 = f32[2,2,2,2,2048]{4,3,2,1,0:T(2,128)S(1)} all-gather(f32[1,2,2,2,2048]{4,3,2,1,0:T(2,128)S(1)} %broadcast_in_dim_reshape.3), channel_id=1, replica_groups=mesh['groups'=2,'seq'=4,'rows'=2,'cfg'=2] {'cfg'}, dimensions={0}, use_global_device_ids=true | all-gather | bytes 196608 | tf_op jit(solution)/shard_map/all_gather | solution.py:84
  13.7 0.1 reshape.50
  13.8 0.1 copy.32
  13.9 0.0 copy-done.7
  14.0 0.2 fusion.10
  14.2 0.1 copy.34
  14.3 0.2 reshape.51
  14.5 4.5 %collective-permute-start = (bf16[2,1,2048]{2,1,0:T(2,128)(2,1)S(1)}, bf16[2,1,2048]{2,1,0:T(2,128)(2,1)S(1)}, u32[]{:S(2)}, u32[]{:S(2)}) collective-permute-start(bf16[2,1,2048]{2,1,0:T(2,128)(2,1)S(1)} %get-tuple-element.36), channel_id=1, source_target_pairs={{0,1},{1,2},{2,3},{4,5},{5,6},{6,7},{8,9},{9,10},{10,11},{12,13},{... | collective-permute-start | bytes 24584 | tf_op jit(solution)/shard_map/ppermute | solution.py:16
  19.0 1.9 %collective-permute-start.1 = (bf16[2,1,2048]{2,1,0:T(2,128)(2,1)S(1)}, bf16[2,1,2048]{2,1,0:T(2,128)(2,1)S(1)}, u32[]{:S(2)}, u32[]{:S(2)}) collective-permute-start(bf16[2,1,2048]{2,1,0:T(2,128)(2,1)S(1)} %get-tuple-element.37), channel_id=1, source_target_pairs={{1,0},{2,1},{3,2},{5,4},{6,5},{7,6},{9,8},{10,9},{11,10},{13,12},{... | collective-permute-start | bytes 24584 | tf_op jit(solution)/shard_map/ppermute | solution.py:19
  21.0 3.1 %collective-permute-done.1 = bf16[2,1,2048]{2,1,0:T(2,128)(2,1)S(1)} collective-permute-done((bf16[2,1,2048]{2,1,0:T(2,128)(2,1)S(1)}, bf16[2,1,2048]{2,1,0:T(2,128)(2,1)S(1)}, u32[]{:S(2)}, u32[]{:S(2)}) %collective-permute-start.1) | collective-permute-done | bytes 8224 | tf_op jit(solution)/shard_map/ppermute | solution.py:19
  24.1 0.1 pad_maximum_fusion
  24.2 3.2 %collective-permute-start.2 = (bf16[2,4,2048]{2,1,0:T(4,128)(2,1)S(1)}, bf16[2,4,2048]{2,1,0:T(4,128)(2,1)S(1)}, u32[]{:S(2)}, u32[]{:S(2)}) collective-permute-start(bf16[2,4,2048]{2,1,0:T(4,128)(2,1)S(1)} %pad_maximum_fusion), channel_id=1, source_target_pairs={{0,4},{4,8},{8,12},{1,5},{5,9},{9,13},{2,6},{6,10},{10,14},{3,7},{... | collective-permute-start | bytes 98312 | tf_op jit(solution)/shard_map/ppermute | solution.py:27
  27.4 1.0 %collective-permute-done.2 = bf16[2,4,2048]{2,1,0:T(4,128)(2,1)S(1)} collective-permute-done((bf16[2,4,2048]{2,1,0:T(4,128)(2,1)S(1)}, bf16[2,4,2048]{2,1,0:T(4,128)(2,1)S(1)}, u32[]{:S(2)}, u32[]{:S(2)}) %collective-permute-start.2) | collective-permute-done | bytes 32800 | tf_op jit(solution)/shard_map/ppermute | solution.py:27
  28.4 0.1 maximum_maximum_fusion
  28.5 0.4 %reshape.52 = bf16[4,4,128,16]{3,2,1,0:T(8,128)(2,1)S(1)} reshape(bf16[4,4,2048]{2,1,0:T(4,128)(2,1)S(1)} %maximum_maximum_fusion) | data formatting | bytes 131072 | tf_op jit(solution)/shard_map/reshape | solution.py:101
  28.8 0.3 pad_slice_fusion.1
  29.1 1.0 %pad_slice_fusion = (bf16[2,2,128,16]{3,2,1,0:T(8,128)(2,1)S(1)}, bf16[2,2,128,16]{3,2,1,0:T(8,128)(2,1)S(1)}, bf16[2,2,128,16]{3,2,1,0:T(8,128)(2,1)S(1)}, bf16...) fusion(bf16[4,4,128,16]{3,2,1,0:T(8,128)(2,1)S(1)} %reshape.52), kind=kLoop, calls=%fused_computation.52 | loop fusion | bytes 819200 | tf_op jit(solution)/shard_map/slice | solution.py:45
  30.1 0.9 %fusion.27 = (bf16[2,2,128,16]{3,2,1,0:T(8,128)(2,1)}, bf16[2,2,128,16]{3,2,1,0:T(8,128)(2,1)}, bf16[2,2,128,16]{3,2,1,0:T(8,128)(2,1)}, bf16[2,2,128,16]{3,2,1,...) fusion(bf16[4,4,128,16]{3,2,1,0:T(8,128)(2,1)S(1)} %reshape.52), kind=kLoop, calls=%fused_computation.70 | loop fusion | bytes 1277952 | tf_op jit(solution)/shard_map/slice | solution.py:45
  31.0 2.9 %concatenate.11 = bf16[2,2,128,432]{3,2,1,0:T(8,128)(2,1)S(1)} concatenate(bf16[2,2,128,16]{3,2,1,0:T(8,128)(2,1)} %get-tuple-element.31, bf16[2,2,128,16]{3,2,1,0:T(8,128)(2,1)} %get-tuple-element.30, bf16[2,2,128,16]{3,2,1,0:T(8,128)(2,1)S(1)} %get-tuple-element.6, bf16[2,2,128,16]{3,2,1,0:T(8,128)(2,1)S(1)} %get-tuple-element.7, bf16[2,2,128,16]{3,2,1,0:T(8,128)(2,1)} %get-tuple-element.29, ...), dimensions={3} | concatenate | bytes 884736 | tf_op jit(solution)/shard_map/concatenate | solution.py:52
  33.9 2.2 %fusion.9 = bf16[512,384]{1,0:T(8,128)(2,1)} fusion(bf16[512,432]{1,0:T(8,128)(2,1)S(1)} %bitcast.55, bf16[432,384]{1,0:T(8,128)(2,1)} %bitcast.58, f32[384]{0:T(512)S(1)} %copy-done.5), kind=kOutput, calls=%fused_computation.12 | convolution fusion | flops 170262528 | bytes 1168896 | tf_op jit(solution)/shard_map/dot_general | solution.py:109
  (22 shorter events, 0.2 us)
Async XLA Ops:
  0.0 7.5 %copy-start = (bf16[5120,64]{0,1:T(8,128)(2,1)S(1)}, bf16[5120,64]{0,1:T(8,128)(2,1)}, u32[]{:S(2)}) copy-start(bf16[5120,64]{0,1:T(8,128)(2,1)} %param.17) | copy-start | bytes 1966084
  0.0 6.6 %copy-start.1 = (bf16[1,256,5120]{2,1,0:T(8,128)(2,1)S(1)}, bf16[1,256,5120]{2,1,0:T(8,128)(2,1)}, u32[]{:S(2)}) copy-start(bf16[1,256,5120]{2,1,0:T(8,128)(2,1)} %param.14) | copy-start | bytes 7864324
  4.4 3.0 %copy-start.3 = (s32[256]{0:T(256)S(1)}, s32[256]{0:T(256)}, u32[]{:S(2)}) copy-start(s32[256]{0:T(256)} %param.15) | copy-start | bytes 3076
  7.5 6.2 %copy-start.2 = (f32[2,2,2048]{2,1,0:T(2,128)S(1)}, f32[2,2,2048]{2,1,0:T(2,128)}, u32[]{:S(2)}) copy-start(f32[2,2,2048]{2,1,0:T(2,128)} %param.16) | copy-start | bytes 98308
  8.6 5.3 %copy-start.4 = (f32[16,16]{1,0:T(8,128)S(1)}, f32[16,16]{1,0:T(8,128)}, u32[]{:S(2)}) copy-start(f32[16,16]{1,0:T(8,128)} %param.24) | copy-start | bytes 3076
  8.7 5.3 %copy-start.6 = (f32[16]{0:T(128)S(1)}, f32[16]{0:T(128)}, u32[]{:S(2)}) copy-start(f32[16]{0:T(128)} %param.25) | copy-start | bytes 196
  8.7 5.3 %copy-start.7 = (f32[16]{0:T(128)S(1)}, f32[16]{0:T(128)}, u32[]{:S(2)}) copy-start(f32[16]{0:T(128)} %param.22) | copy-start | bytes 196
  8.7 5.3 %copy-start.8 = (f32[16]{0:T(128)S(1)}, f32[16]{0:T(128)}, u32[]{:S(2)}) copy-start(f32[16]{0:T(128)} %param.23) | copy-start | bytes 196
  14.5 6.4 %collective-permute-start = (bf16[2,1,2048]{2,1,0:T(2,128)(2,1)S(1)}, bf16[2,1,2048]{2,1,0:T(2,128)(2,1)S(1)}, u32[]{:S(2)}, u32[]{:S(2)}) collective-permute-start(bf16[2,1,2048]{2,1,0:T(2,128)(2,1)S(1)} %get-tuple-element.36), channel_id=1, source_target_pairs={{0,1},{1,2},{2,3},{4,5},{5,6},{6,7},{8,9},{9,10},{10,11},{12,13},{... | collective-permute-start | bytes 24584 | tf_op jit(solution)/shard_map/ppermute | solution.py:16
  19.0 5.1 %collective-permute-start.1 = (bf16[2,1,2048]{2,1,0:T(2,128)(2,1)S(1)}, bf16[2,1,2048]{2,1,0:T(2,128)(2,1)S(1)}, u32[]{:S(2)}, u32[]{:S(2)}) collective-permute-start(bf16[2,1,2048]{2,1,0:T(2,128)(2,1)S(1)} %get-tuple-element.37), channel_id=1, source_target_pairs={{1,0},{2,1},{3,2},{5,4},{6,5},{7,6},{9,8},{10,9},{11,10},{13,12},{... | collective-permute-start | bytes 24584 | tf_op jit(solution)/shard_map/ppermute | solution.py:19
  24.2 4.2 %collective-permute-start.2 = (bf16[2,4,2048]{2,1,0:T(4,128)(2,1)S(1)}, bf16[2,4,2048]{2,1,0:T(4,128)(2,1)S(1)}, u32[]{:S(2)}, u32[]{:S(2)}) collective-permute-start(bf16[2,4,2048]{2,1,0:T(4,128)(2,1)S(1)} %pad_maximum_fusion), channel_id=1, source_target_pairs={{0,4},{4,8},{8,12},{1,5},{5,9},{9,13},{2,6},{6,10},{10,14},{3,7},{... | collective-permute-start | bytes 98312 | tf_op jit(solution)/shard_map/ppermute | solution.py:27
  30.1 3.8 %copy-start.5 = (f32[384]{0:T(512)S(1)}, f32[384]{0:T(512)}, u32[]{:S(2)}) copy-start(f32[384]{0:T(512)} %param.27) | copy-start | bytes 4612
where the time goes:
time: 36.6 us; the launch traced here: 36.1 us
  local copies, waits for them, and re-layouts  9.76 us (27%)
  starting transfers between devices  9.62 us (26%)
  waiting for transfers between devices  4.13 us (11%)
  other arithmetic  4.12 us (11%)
  matrix products  3.55 us (10%)
  between operations  2.99 us (8%)
  blocking collectives  1.9 us (5%)
    ppermute x1, starting transfers between devices, padded_2(): lax.ppermute(lax.slice_in_dim(block, block.shape[dim] - width, None, axis...  4.5 us
    ppermute x1, starting transfers between devices, shifted(): return lax.ppermute(block, axis, route)  3.2 us
    ppermute x1, waiting for transfers between devices, padded_2(): lax.ppermute(lax.slice_in_dim(block, 0, width, axis=dim), axis, backward)  3.12 us
    concatenate x1, local copies, waits for them, and re-layouts, conv_taps(): return jnp.concatenate(pieces, axis=-1)  2.88 us
    reduce_sum x1, other arithmetic, head_rows(): center = jnp.mean(values, axis=-1, keepdims=True)  2.18 us
    slice x3, local copies, waits for them, and re-layouts, conv_taps(): padded[step_time:step_time + frames, step_row:step_row + row_count, step_...  2.17 us
    dot_general x1, matrix products, per_device(): jnp.dot(tap_columns, kernel, preferred_element_type=jnp.float32)  2.16 us
    ppermute x1, starting transfers between devices, padded_2(): lax.ppermute(lax.slice_in_dim(block, 0, width, axis=dim), axis, backward)  1.92 us
  transfers between devices with their start and end apart: 3, of which 2 were waited for; matrix products, arithmetic and copies ran while one was open for 0% of the time, Pallas kernels for 0%

commit v1 on v0

--- a/solution.py
+++ b/solution.py
@@ -81,7 +81,9 @@
     placed = jnp.zeros((token_count, patch_width), jnp.float32).at[local_cell].set(own_head)
     local_block = placed.reshape(FR_DEV, TR_DEV, WT, 2, 2, lat_channels).transpose(0, 1, 3, 2, 4, 5)
     local_block = local_block.reshape(FR_DEV, 2, TR_DEV, 2 * WT * lat_channels)
-    gathered = lax.all_gather(local_block[None], "cfg", axis=0, tiled=True)
+    gathered = jnp.concatenate(
+        lax.all_to_all(jnp.stack([local_block[None]] * lax.axis_size("cfg")), "cfg", 0, 0), axis=0
+    )
     half_index = lax.axis_index("cfg")
     conditional = lax.dynamic_index_in_dim(gathered[0], half_index, 1, keepdims=False)
     unconditional = lax.dynamic_index_in_dim(gathered[1], half_index, 1, keepdims=False)

time: 36.6 us -> 38.1 us (1.041)
  starting transfers between devices: 9.62 us -> 13 us
  blocking collectives: 1.9 us -> 0 us
  other arithmetic: 4.12 us -> 4.94 us
  local copies, waits for them, and re-layouts: 9.76 us -> 9.05 us
    all_to_all x0 -> x1, starting transfers between devices: none -> 3.39 us  [per_device(): lax.all_to_all(jnp.stack([local_block[None]] * lax.axis_size('cfg')), 'cf...]
    all_gather x1 -> x0, blocking collectives: 1.9 us -> none  [per_device(): gathered = lax.all_gather(local_block[None], 'cfg', axis=0, tiled=True)]
    dynamic_slice x1, local copies, waits for them, and re-layouts: 1.39 us -> 0.65 us  [per_device(): sigma_now = step_table[step_index].astype(jnp.float32) / 1000.0]
    another operation x0 -> x1, other arithmetic: none -> 0.7 us  [per_device(): jnp.stack([local_block[None]] * lax.axis_size('cfg'))]
  transfers between devices with their start and end apart: 3 -> 4, of which waited for: 2 -> 2; matrix products, arithmetic and copies ran while one was open for 0% -> 2% of each run, Pallas kernels for 0% -> 0%
where the time goes in v1:
time: 38.1 us; the launch traced here: 37.5 us
  starting transfers between devices  13 us (34%)
  local copies, waits for them, and re-layouts  9.05 us (24%)
  other arithmetic  4.94 us (13%)
  waiting for transfers between devices  4.13 us (11%)
  matrix products  3.56 us (9%)
  between operations  2.85 us (7%)
    ppermute x1, starting transfers between devices, padded_2(): lax.ppermute(lax.slice_in_dim(block, block.shape[dim] - width, None, axis...  4.5 us
    all_to_all x1, starting transfers between devices, per_device(): lax.all_to_all(jnp.stack([local_block[None]] * lax.axis_size('cfg')), 'cf...  3.39 us
    ppermute x1, starting transfers between devices, shifted(): return lax.ppermute(block, axis, route)  3.2 us
    ppermute x1, waiting for transfers between devices, padded_2(): lax.ppermute(lax.slice_in_dim(block, 0, width, axis=dim), axis, backward)  3.12 us
    concatenate x1, local copies, waits for them, and re-layouts, conv_taps(): return jnp.concatenate(pieces, axis=-1)  2.88 us
    reduce_sum x1, other arithmetic, head_rows(): center = jnp.mean(values, axis=-1, keepdims=True)  2.21 us
    slice x3, local copies, waits for them, and re-layouts, conv_taps(): padded[step_time:step_time + frames, step_row:step_row + row_count, step_...  2.18 us
    dot_general x1, matrix products, per_device(): jnp.dot(tap_columns, kernel, preferred_element_type=jnp.float32)  2.16 us
  transfers between devices with their start and end apart: 4, of which 2 were waited for; matrix products, arithmetic and copies ran while one was open for 2% of the time, Pallas kernels for 0%

profile of v1, /device:TPU:1, one launch (start us, length us, event | category | flops | bytes accessed | tf_op | source)
XLA Modules:
  0.0 37.5 jit_solution(14054765211921625573)
XLA Ops:
  0.0 1.0 %slice_add_fusion = (f32[1,5120]{1,0:T(1,128)S(1)}, f32[1,5120]{1,0:T(1,128)S(1)}) fusion(f32[2,5120]{1,0:T(2,128)} %param.18), kind=kLoop, calls=%fused_computation.27 | loop fusion | flops 5120 | bytes 81920 | tf_op jit(solution)/shard_map/add | solution.py:35
  1.0 2.2 %convert_reduce_fusion = f32[256]{0:T(256)S(1)} fusion(bf16[1,256,5120]{2,1,0:T(8,128)(2,1)} %param.14), kind=kLoop, calls=%fused_computation.1 | loop fusion | flops 2621184 | bytes 2622464 | tf_op jit(solution)/shard_map/reduce_sum | solution.py:32
  3.2 0.8 %fusion.3 = f32[256]{0:T(256)S(1)} fusion(bf16[1,256,5120]{2,1,0:T(8,128)(2,1)S(1)} %copy-done.1, f32[256]{0:T(256)S(1)} %broadcast_multiply_fusion), kind=kLoop, calls=%fused_computation.6 | loop fusion | flops 5242624 | bytes 2623488 | tf_op jit(solution)/shard_map/reduce_sum | solution.py:33
  4.1 0.0 copy-start.3
  4.2 1.2 %fusion.7 = f32[256,64]{1,0:T(8,128)S(1)} fusion(bf16[5120,64]{0,1:T(8,128)(2,1)S(1)} %copy-done, bf16[1,256,5120]{2,1,0:T(8,128)(2,1)S(1)} %copy-done.1, f32[5120]{0:T(1024)S(1)} %bitcast.57, f32[5120]{0:T(1024)S(1)} %bitcast.56, f32[256]{0:T(256)S(1)} %add_rsqrt_fusion, f32[256]{0:T(256)S(1)} %broadcast_multiply_fusion), kind=kOutput, calls=%fused_computation.10 | convolution fusion | flops 175636480 | bytes 3385344 | tf_op jit(solution)/shard_map/dot_general | solution.py:36
  5.4 1.2 %scatter_custom_fusion = f32[256,64]{1,0:T(8,128)S(1)} fusion(s32[256]{0:T(256)S(1)} %compare_select_fusion, f32[256,64]{1,0:T(8,128)S(1)} %fusion.7, f32[]{:T(128)} %constant.82.clone.1), kind=kCustom, calls=%fused_computation.17 | custom fusion | bytes 65540 | tf_op jit(solution)/shard_map/scatter | solution.py:81
  6.6 0.1 copy.24
  6.6 0.1 reshape.54
  6.8 0.3 copy.25
  7.0 0.7 %stack_broadcast_in_dim_reshape.4 = f32[1,1,2,2,2,2048]{5,4,3,2,1,0:T(2,128)S(1)} reshape(f32[2,2,2,64,2,16]{5,4,3,2,1,0:T(2,128)S(1)} %copy.25) | data formatting | bytes 131072 | tf_op jit(solution)/shard_map/stack;broadcast_in_dim;reshape | solution.py:85
  7.7 0.7 %pad_maximum_fusion = f32[2,1,2,2,2,2048]{5,4,3,2,1,0:T(2,128)} fusion(f32[1,1,2,2,2,2048]{5,4,3,2,1,0:T(2,128)S(1)} %stack_broadcast_in_dim_reshape.4), kind=kLoop, calls=%fused_computation.15 | loop fusion | flops 32768 | bytes 196608 | tf_op jit(solution)/shard_map/stack | solution.py:85
  8.4 3.4 %all-to-all-start = ((f32[2,1,2,2,2,2048]{5,4,3,2,1,0:T(2,128)}), f32[2,1,2,2,2,2048]{5,4,3,2,1,0:T(2,128)S(1)}, u32[]{:S(2)}, u32[]{:S(2)}) async-start(f32[2,1,2,2,2,2048]{5,4,3,2,1,0:T(2,128)} %pad_maximum_fusion), calls=%async_computation | async-start | bytes 262144 | tf_op jit(solution)/shard_map/all_to_all | solution.py:85
  12.5 0.7 %fusion.30 = (s32[1]{0:T(128)}, s32[1]{0:T(128)}) fusion(s32[9]{0:T(128)S(1)} %copy-done.3, s32[]{:T(128)S(6)} %select_n.38, s32[]{:T(128)S(6)} %select_n.37), kind=kLoop, calls=%fused_computation.74 | loop fusion | bytes 24 | tf_op jit(solution)/shard_map/dynamic_slice | solution.py:92
  15.1 0.1 reshape.55
  15.3 0.1 copy.26
  15.4 0.0 copy-done.8
  15.4 0.2 fusion.10
  15.7 0.1 copy.28
  15.8 0.2 reshape.56
  16.0 4.5 %collective-permute-start = (bf16[2,1,2048]{2,1,0:T(2,128)(2,1)S(1)}, bf16[2,1,2048]{2,1,0:T(2,128)(2,1)S(1)}, u32[]{:S(2)}, u32[]{:S(2)}) collective-permute-start(bf16[2,1,2048]{2,1,0:T(2,128)(2,1)S(1)} %get-tuple-element.36), channel_id=1, source_target_pairs={{0,1},{1,2},{2,3},{4,5},{5,6},{6,7},{8,9},{9,10},{10,11},{12,13},{... | collective-permute-start | bytes 24584 | tf_op jit(solution)/shard_map/ppermute | solution.py:16
  20.5 1.9 %collective-permute-start.1 = (bf16[2,1,2048]{2,1,0:T(2,128)(2,1)S(1)}, bf16[2,1,2048]{2,1,0:T(2,128)(2,1)S(1)}, u32[]{:S(2)}, u32[]{:S(2)}) collective-permute-start(bf16[2,1,2048]{2,1,0:T(2,128)(2,1)S(1)} %get-tuple-element.37), channel_id=1, source_target_pairs={{1,0},{2,1},{3,2},{5,4},{6,5},{7,6},{9,8},{10,9},{11,10},{13,12},{... | collective-permute-start | bytes 24584 | tf_op jit(solution)/shard_map/ppermute | solution.py:19
  22.4 3.1 %collective-permute-done.1 = bf16[2,1,2048]{2,1,0:T(2,128)(2,1)S(1)} collective-permute-done((bf16[2,1,2048]{2,1,0:T(2,128)(2,1)S(1)}, bf16[2,1,2048]{2,1,0:T(2,128)(2,1)S(1)}, u32[]{:S(2)}, u32[]{:S(2)}) %collective-permute-start.1) | collective-permute-done | bytes 8224 | tf_op jit(solution)/shard_map/ppermute | solution.py:19
  25.6 0.1 pad_maximum_fusion.1
  25.6 3.2 %collective-permute-start.2 = (bf16[2,4,2048]{2,1,0:T(4,128)(2,1)S(1)}, bf16[2,4,2048]{2,1,0:T(4,128)(2,1)S(1)}, u32[]{:S(2)}, u32[]{:S(2)}) collective-permute-start(bf16[2,4,2048]{2,1,0:T(4,128)(2,1)S(1)} %pad_maximum_fusion.1), channel_id=1, source_target_pairs={{0,4},{4,8},{8,12},{1,5},{5,9},{9,13},{2,6},{6,10},{10,14},{3,7},{... | collective-permute-start | bytes 98312 | tf_op jit(solution)/shard_map/ppermute | solution.py:27
  28.8 1.0 %collective-permute-done.2 = bf16[2,4,2048]{2,1,0:T(4,128)(2,1)S(1)} collective-permute-done((bf16[2,4,2048]{2,1,0:T(4,128)(2,1)S(1)}, bf16[2,4,2048]{2,1,0:T(4,128)(2,1)S(1)}, u32[]{:S(2)}, u32[]{:S(2)}) %collective-permute-start.2) | collective-permute-done | bytes 32800 | tf_op jit(solution)/shard_map/ppermute | solution.py:27
  29.8 0.1 maximum_maximum_fusion
  29.9 0.4 reshape.57
  30.3 0.3 pad_slice_fusion.1
  30.6 1.0 %pad_slice_fusion = (bf16[2,2,128,16]{3,2,1,0:T(8,128)(2,1)S(1)}, bf16[2,2,128,16]{3,2,1,0:T(8,128)(2,1)S(1)}, bf16[2,2,128,16]{3,2,1,0:T(8,128)(2,1)S(1)}, bf16...) fusion(bf16[4,4,128,16]{3,2,1,0:T(8,128)(2,1)S(1)} %reshape.57), kind=kLoop, calls=%fused_computation.53 | loop fusion | bytes 819200 | tf_op jit(solution)/shard_map/slice | solution.py:45
  31.6 0.9 %fusion.27 = (bf16[2,2,128,16]{3,2,1,0:T(8,128)(2,1)}, bf16[2,2,128,16]{3,2,1,0:T(8,128)(2,1)}, bf16[2,2,128,16]{3,2,1,0:T(8,128)(2,1)}, bf16[2,2,128,16]{3,2,1,...) fusion(bf16[4,4,128,16]{3,2,1,0:T(8,128)(2,1)S(1)} %reshape.57), kind=kLoop, calls=%fused_computation.71 | loop fusion | bytes 1277952 | tf_op jit(solution)/shard_map/slice | solution.py:45
  32.5 2.9 %concatenate.11 = bf16[2,2,128,432]{3,2,1,0:T(8,128)(2,1)S(1)} concatenate(bf16[2,2,128,16]{3,2,1,0:T(8,128)(2,1)} %get-tuple-element.31, bf16[2,2,128,16]{3,2,1,0:T(8,128)(2,1)} %get-tuple-element.30, bf16[2,2,128,16]{3,2,1,0:T(8,128)(2,1)S(1)} %get-tuple-element.6, bf16[2,2,128,16]{3,2,1,0:T(8,128)(2,1)S(1)} %get-tuple-element.7, bf16[2,2,128,16]{3,2,1,0:T(8,128)(2,1)} %get-tuple-element.29, ...), dimensions={3} | concatenate | bytes 884736 | tf_op jit(solution)/shard_map/concatenate | solution.py:52
  35.4 2.2 %fusion.9 = bf16[512,384]{1,0:T(8,128)(2,1)} fusion(bf16[512,432]{1,0:T(8,128)(2,1)S(1)} %bitcast.55, bf16[432,384]{1,0:T(8,128)(2,1)} %bitcast.58, f32[384]{0:T(512)S(1)} %copy-done.6), kind=kOutput, calls=%fused_computation.12 | convolution fusion | flops 170262528 | bytes 1168896 | tf_op jit(solution)/shard_map/dot_general | solution.py:111
  (26 shorter events, 0.2 us)
Async XLA Ops:
  0.0 4.1 %copy-start = (bf16[5120,64]{0,1:T(8,128)(2,1)S(1)}, bf16[5120,64]{0,1:T(8,128)(2,1)}, u32[]{:S(2)}) copy-start(bf16[5120,64]{0,1:T(8,128)(2,1)} %param.17) | copy-start | bytes 1966084
  0.0 3.2 %copy-start.1 = (bf16[1,256,5120]{2,1,0:T(8,128)(2,1)S(1)}, bf16[1,256,5120]{2,1,0:T(8,128)(2,1)}, u32[]{:S(2)}) copy-start(bf16[1,256,5120]{2,1,0:T(8,128)(2,1)} %param.14) | copy-start | bytes 7864324
  1.0 3.1 %copy-start.4 = (s32[256]{0:T(256)S(1)}, s32[256]{0:T(256)}, u32[]{:S(2)}) copy-start(s32[256]{0:T(256)} %param.15) | copy-start | bytes 3076
  4.1 8.4 %copy-start.3 = (s32[9]{0:T(128)S(1)}, s32[9]{0:T(128)}, u32[]{:S(2)}) copy-start(s32[9]{0:T(128)} %param.21) | copy-start | bytes 112
  4.1 10.9 %copy-start.2 = (f32[2,2,2048]{2,1,0:T(2,128)S(1)}, f32[2,2,2048]{2,1,0:T(2,128)}, u32[]{:S(2)}) copy-start(f32[2,2,2048]{2,1,0:T(2,128)} %param.16) | copy-start | bytes 98308
  5.3 10.1 %copy-start.5 = (f32[16,16]{1,0:T(8,128)S(1)}, f32[16,16]{1,0:T(8,128)}, u32[]{:S(2)}) copy-start(f32[16,16]{1,0:T(8,128)} %param.24) | copy-start | bytes 3076
  5.3 10.1 %copy-start.7 = (f32[16]{0:T(128)S(1)}, f32[16]{0:T(128)}, u32[]{:S(2)}) copy-start(f32[16]{0:T(128)} %param.25) | copy-start | bytes 196
  5.3 10.1 %copy-start.8 = (f32[16]{0:T(128)S(1)}, f32[16]{0:T(128)}, u32[]{:S(2)}) copy-start(f32[16]{0:T(128)} %param.22) | copy-start | bytes 196
  5.3 10.1 %copy-start.9 = (f32[16]{0:T(128)S(1)}, f32[16]{0:T(128)}, u32[]{:S(2)}) copy-start(f32[16]{0:T(128)} %param.23) | copy-start | bytes 196
  8.4 6.6 %all-to-all-start = ((f32[2,1,2,2,2,2048]{5,4,3,2,1,0:T(2,128)}), f32[2,1,2,2,2,2048]{5,4,3,2,1,0:T(2,128)S(1)}, u32[]{:S(2)}, u32[]{:S(2)}) async-start(f32[2,1,2,2,2,2048]{5,4,3,2,1,0:T(2,128)} %pad_maximum_fusion), calls=%async_computation | async-start | bytes 262144 | tf_op jit(solution)/shard_map/all_to_all | solution.py:85
  16.0 6.4 %collective-permute-start = (bf16[2,1,2048]{2,1,0:T(2,128)(2,1)S(1)}, bf16[2,1,2048]{2,1,0:T(2,128)(2,1)S(1)}, u32[]{:S(2)}, u32[]{:S(2)}) collective-permute-start(bf16[2,1,2048]{2,1,0:T(2,128)(2,1)S(1)} %get-tuple-element.36), channel_id=1, source_target_pairs={{0,1},{1,2},{2,3},{4,5},{5,6},{6,7},{8,9},{9,10},{10,11},{12,13},{... | collective-permute-start | bytes 24584 | tf_op jit(solution)/shard_map/ppermute | solution.py:16
  20.5 5.1 %collective-permute-start.1 = (bf16[2,1,2048]{2,1,0:T(2,128)(2,1)S(1)}, bf16[2,1,2048]{2,1,0:T(2,128)(2,1)S(1)}, u32[]{:S(2)}, u32[]{:S(2)}) collective-permute-start(bf16[2,1,2048]{2,1,0:T(2,128)(2,1)S(1)} %get-tuple-element.37), channel_id=1, source_target_pairs={{1,0},{2,1},{3,2},{5,4},{6,5},{7,6},{9,8},{10,9},{11,10},{13,12},{... | collective-permute-start | bytes 24584 | tf_op jit(solution)/shard_map/ppermute | solution.py:19
  25.6 4.2 %collective-permute-start.2 = (bf16[2,4,2048]{2,1,0:T(4,128)(2,1)S(1)}, bf16[2,4,2048]{2,1,0:T(4,128)(2,1)S(1)}, u32[]{:S(2)}, u32[]{:S(2)}) collective-permute-start(bf16[2,4,2048]{2,1,0:T(4,128)(2,1)S(1)} %pad_maximum_fusion.1), channel_id=1, source_target_pairs={{0,4},{4,8},{8,12},{1,5},{5,9},{9,13},{2,6},{6,10},{10,14},{3,7},{... | collective-permute-start | bytes 98312 | tf_op jit(solution)/shard_map/ppermute | solution.py:27
  31.6 3.8 %copy-start.6 = (f32[384]{0:T(512)S(1)}, f32[384]{0:T(512)}, u32[]{:S(2)}) copy-start(f32[384]{0:T(512)} %param.27) | copy-start | bytes 4612
